TPU v7x, 32 devices: a whole 2x2x4 slice. The times are simulated.
32 devices in a mesh: row: 8 (over y, x, core), col: 4 (over z).
Axes of the slice: x: 2, y: 2, z: 4, core: 2. Of those that a mesh axis runs over, the one named last changes fastest.
Arguments:
- col_samples: float32 [16, 2, 2048, 128], P('row', None, 'col'), may hold values from -6 to 6
- row_samples: float32 [16, 2, 128, 2048], P('row', None, None, 'col'), may hold values from -6 to 6
- pivot_rows: int32 [16, 128], P('row'), may hold values from 0 to 2047
- rank_blocks: int32 [16], P('row'), may hold values from 1 to 8
- upper_inverse: float32 [2, 2048, 2048], P(None, 'col', 'row'), as said below
- upanel_left: float32 [4, 2, 2048, 128], P('col'), may hold values from -0.125 to 0.125
Outputs:
- panel_right: float32 [16, 2, 128, 2048], P('row', None, None, 'col')
- cores: float32 [16, 4, 2, 128, 128], P('row', 'col')
Inputs may be any that keep to these rules, and one draw needn't show every extreme that they name: `rank_blocks`: the tile's rank is 16 times this. `upper_inverse`: zero below the diagonal in both parts.
All inputs are finite; a program needn't handle non-finite values.
Results may differ from a plain program's by a relative error of at most 0.00007.
Values sent between devices are 32-bit elements; how exact they have to be, the bound alone decides.
A program may use at most 64 MiB of HBM per device.

v0:
```python
import jax
import jax.numpy as jnp
from jax import lax
from jax.sharding import PartitionSpec as P

RANK_STEP = 16


def complex_product(pattern, left_real, left_imag, right_real, right_imag):

    def single(left, right):
        return jnp.einsum(
            pattern,
            left,
            right,
            precision=lax.Precision.HIGHEST,
            preferred_element_type=jnp.float32,
        )

    real_part = single(left_real, right_real) - single(left_imag, right_imag)
    imag_part = single(left_real, right_imag) + single(left_imag, right_real)
    return (real_part, imag_part)


def scale_rows(values, weight_real, weight_imag):
    wr = weight_real[:, :, None]
    wi = weight_imag[:, :, None]
    real_part = values[:, 0] * wr - values[:, 1] * wi
    imag_part = values[:, 0] * wi + values[:, 1] * wr
    return jnp.stack((real_part, imag_part), axis=1)


def on_device(col_samples, row_samples, pivot_rows, rank_blocks, upper_inverse, upanel_left):
    width_local = col_samples.shape[2]
    ranks_max = row_samples.shape[2]
    offset = lax.axis_index("col") * width_local
    positions = offset + lax.broadcasted_iota(jnp.int32, (1, 1, width_local), 2)
    hits = (pivot_rows[:, :, None] == positions).astype(jnp.float32)
    flipped = jnp.swapaxes(col_samples, 2, 3)
    partial_entries = jnp.sum(flipped * hits[:, None], axis=3)
    entries = lax.psum(partial_entries, "col")
    levels = lax.broadcasted_iota(jnp.int32, (1, ranks_max), 1)
    keeping = (levels < RANK_STEP * rank_blocks[:, None]).astype(jnp.float32)
    magnitude = jnp.maximum(entries[:, 0] * entries[:, 0] + entries[:, 1] * entries[:, 1], 1.0)
    factor_real = keeping * entries[:, 0] / magnitude
    factor_imag = -keeping * entries[:, 1] / magnitude
    scaled = scale_rows(row_samples, factor_real, factor_imag)
    portion = lax.all_gather(upper_inverse, "row", axis=2, tiled=True)
    real_part, imag_part = complex_product(
        "trk,kn->trn", scaled[:, 0], scaled[:, 1], portion[0], portion[1]
    )
    partial_panel = jnp.stack((real_part, imag_part), axis=1)
    panel_full = lax.psum(partial_panel, "col")
    core_real, core_imag = complex_product(
        "trn,jns->tjrs", panel_full[:, 0], panel_full[:, 1], upanel_left[:, 0], upanel_left[:, 1]
    )
    cores = jnp.stack((core_real, core_imag), axis=2)
    panel_local = lax.dynamic_slice_in_dim(panel_full, offset, width_local, 3)
    return (panel_local, cores)


def solution(mesh):
    in_specs = (
        P("row", None, "col", None),
        P("row", None, None, "col"),
        P("row", None),
        P("row"),
        P(None, "col", "row"),
        P("col", None, None, None),
    )
    out_specs = (P("row", None, None, "col"), P("row", "col", None, None, None))
    return jax.shard_map(
        on_device, mesh=mesh, in_specs=in_specs, out_specs=out_specs, check_vma=False
    )
```

profile of v0, /device:TPU:0, one launch (start us, length us, event | category | flops | bytes accessed | tf_op | source)
XLA Modules:
  0.0 263.2 jit_solution(7308855048611063219)
XLA Ops:
  7.2 0.0 all-gather.2.cloned.1.call-start
  7.2 0.7 all-gather.2.cloned.1.call-update
  7.9 0.0 all-reduce.2.cloned.1.call-start
  8.0 0.8 compare_convert_fusion
  8.8 0.0 copy-start.3
  8.8 1.4 fusion.20
  10.2 13.5 %psum.14 = f32[2,2,128]{2,1,0:T(2,128)S(1)} all-reduce(f32[2,2,128]{2,1,0:T(2,128)S(1)} %fusion.20), channel_id=1, replica_groups=mesh['row'=8,'col'=4] {'col'}, use_global_device_ids=true, to_apply=%region_1.0 | all-reduce | flops 512 | bytes 4096 | tf_op jit(solution)/shard_map/psum | solution.py:41
  23.7 0.7 broadcast_multiply_fusion
  24.3 0.1 select_divide_fusion
  24.4 44.1 %all-gather.2.cloned.1.call-done = f32[2,512,2048]{2,1,0:T(8,128)} async-done(((f32[2,512,256]{2,1,0:T(8,128)}), f32[2,512,2048]{2,1,0:T(8,128)}) %all-gather.2.cloned.1.call-update) | async-done | bytes 8388624 | tf_op jit(solution)/shard_map/all_gather | solution.py:48
  68.5 0.0 copy-start
  68.5 5.9 %fusion = f32[2,128,2048]{2,1,0:T(8,128)S(1)} fusion(f32[2,512,2048]{2,1,0:T(8,128)} %all-gather.2.cloned.1.call-done, f32[2,2,128,512]{3,2,1,0:T(8,128)} %param.7, f32[2,128]{1,0:T(2,128)S(1)} %get-tuple-element.7, f32[2,128]{1,0:T(2,128)S(1)} %get-tuple-element.6), kind=kOutput, calls=%fused_computation.3 | convolution fusion | flops 3221618688 | bytes 7342080 | tf_op jit(solution)/shard_map/trk,kn->trn/dot_general | solution.py:12
  74.4 0.0 copy-done.3
  74.4 5.7 %fusion.1 = f32[2,128,2048]{2,1,0:T(8,128)S(1)} fusion(f32[2,512,2048]{2,1,0:T(8,128)} %all-gather.2.cloned.1.call-done, f32[2,2,128,512]{3,2,1,0:T(8,128)S(1)} %copy-done.3, f32[2,128]{1,0:T(2,128)S(1)} %get-tuple-element.7, f32[2,128]{1,0:T(2,128)S(1)} %get-tuple-element.6), kind=kOutput, calls=%fused_computation.4 | convolution fusion | flops 3221618688 | bytes 7342080 | tf_op jit(solution)/shard_map/trk,kn->trn/dot_general | solution.py:12
  80.1 0.0 copy-done
  80.1 3.8 %fusion.7 = f32[2,1,128,2048]{3,2,0,1:T(8,128)S(1)} fusion(f32[2,128,2048]{2,1,0:T(8,128)S(1)} %fusion, f32[2,512,2048]{2,1,0:T(8,128)S(1)} %copy-done, f32[2,2,128,512]{3,2,1,0:T(8,128)S(1)} %copy-done.3, f32[2,128]{1,0:T(2,128)S(1)} %get-tuple-element.7, f32[2,128]{1,0:T(2,128)S(1)} %get-tuple-element.6), kind=kOutput, calls=%fused_computation.10 | convolution fusion | flops 3222142976 | bytes 9439232 | tf_op jit(solution)/shard_map/trk,kn->trn/dot_general | solution.py:12
  84.0 3.8 %fusion.5 = f32[2,1,128,2048]{3,2,0,1:T(8,128)S(1)} fusion(f32[2,128,2048]{2,1,0:T(8,128)S(1)} %fusion.1, f32[2,512,2048]{2,1,0:T(8,128)S(1)} %copy-done, f32[2,2,128,512]{3,2,1,0:T(8,128)S(1)} %copy-done.3, f32[2,128]{1,0:T(2,128)S(1)} %get-tuple-element.7, f32[2,128]{1,0:T(2,128)S(1)} %get-tuple-element.6), kind=kOutput, calls=%fused_computation.8 | convolution fusion | flops 3222142976 | bytes 9439232 | tf_op jit(solution)/shard_map/trk,kn->trn/dot_general | solution.py:12
  87.8 2.5 pad_maximum_fusion
  90.2 0.0 copy-start.2
  90.2 0.0 all-reduce.2.cloned.1.call-update
  90.3 155.1 %all-reduce.2.cloned.1.call-done = f32[2,2,128,2048]{3,2,0,1:T(8,128)} async-done(((f32[2,2,128,2048]{3,2,0,1:T(8,128)}), f32[2,2,128,2048]{3,2,0,1:T(8,128)}) %all-reduce.2.cloned.1.call-update) | async-done | bytes 4194320 | tf_op jit(solution)/shard_map/psum | solution.py:53
  245.4 0.0 copy-start.1
  245.4 1.4 constant_dynamic-slice_fusion
  246.8 1.0 copy.11
  247.9 0.0 copy-done.2
  247.9 0.1 copy-done.1
  248.0 1.8 fusion.8
  249.8 1.8 fusion.9
  251.7 2.1 fusion.15
  253.8 1.8 fusion.13
  255.6 0.7 copy.12
  (3 shorter events, 0.0 us)
Async XLA Ops:
  7.2 61.3 %all-gather.2.cloned.1.call-start = ((), (), s32[]{:S(2)}) async-start(), calls=%async_computation | async-start | bytes 9437184 | tf_op jit(solution)/shard_map/all_gather | solution.py:48
  7.9 237.5 %all-reduce.2.cloned.1.call-start = ((), (), s32[]{:S(2)}) async-start(), calls=%async_computation.1 | async-start | bytes 8388608 | tf_op jit(solution)/shard_map/psum | solution.py:53
  8.8 65.6 %copy-start.3 = (f32[2,2,128,512]{3,2,1,0:T(8,128)S(1)}, f32[2,2,128,512]{3,2,1,0:T(8,128)}, u32[]{:S(2)}) copy-start(f32[2,2,128,512]{3,2,1,0:T(8,128)} %param.7) | copy-start | bytes 3145732
  68.5 11.7 %copy-start = (f32[2,512,2048]{2,1,0:T(8,128)S(1)}, f32[2,512,2048]{2,1,0:T(8,128)}, u32[]{:S(2)}) copy-start(f32[2,512,2048]{2,1,0:T(8,128)} %all-gather.2.cloned.1.call-done) | copy-start | bytes 25165828
  90.2 157.6 %copy-start.2 = (f32[1,2,2048,128]{3,2,1,0:T(8,128)S(1)}, f32[1,2,2048,128]{3,2,1,0:T(8,128)}, u32[]{:S(2)}) copy-start(f32[1,2,2048,128]{3,2,1,0:T(8,128)} %param.11) | copy-start | bytes 6291460
  245.4 2.6 copy-start.1
Sparse Core Ops, SparseCore 0:
  9.8 58.5 all-gather.1
  90.4 154.9 all-reduce.1
where the time goes:
time: 263 us
  waiting for transfers between devices  200 us (76%)
  matrix products  26.8 us (10%)
  between operations  14.2 us (5%)
  blocking collectives  13.5 us (5%)
  other arithmetic  5.43 us (2%)
  local copies, waits for them, and re-layouts  3.36 us (1%)
    psum x1, waiting for transfers between devices, on_device(): panel_full = lax.psum(partial_panel, 'col')  155 us
    all_gather x1, waiting for transfers between devices, on_device(): portion = lax.all_gather(upper_inverse, 'row', axis=2, tiled=True)  44.1 us
    dot_general x8, matrix products, single(): jnp.einsum(pattern, left, right, precision=lax.Precision.HIGHEST, preferr...  26.8 us
    psum x1, blocking collectives, on_device(): entries = lax.psum(partial_entries, 'col')  13.5 us
  transfers between devices with their start and end apart: 2, of which 2 were waited for; matrix products, arithmetic and copies ran while one was open for 1% of the time, Pallas kernels for 0%

commit v1 on v0

--- a/solution.py
+++ b/solution.py
@@ -50,7 +50,8 @@
         "trk,kn->trn", scaled[:, 0], scaled[:, 1], portion[0], portion[1]
     )
     partial_panel = jnp.stack((real_part, imag_part), axis=1)
-    panel_full = lax.psum(partial_panel, "col")
+    pieces = lax.all_gather(partial_panel, "col", axis=0, tiled=False)
+    panel_full = pieces.sum(axis=0)
     core_real, core_imag = complex_product(
         "trn,jns->tjrs", panel_full[:, 0], panel_full[:, 1], upanel_left[:, 0], upanel_left[:, 1]
     )

time: 263 us -> 407 us (1.55)
  waiting for transfers between devices: 200 us -> 332 us
  other arithmetic: 5.43 us -> 15.7 us
    all_gather x0 -> x1, waiting for transfers between devices: none -> 287 us  [on_device(): pieces = lax.all_gather(partial_panel, 'col', axis=0, tiled=False)]
    psum x1 -> x0, waiting for transfers between devices: 155 us -> none  [on_device(): panel_full = lax.psum(partial_panel, 'col')]
    reduce_sum x0 -> x1, other arithmetic: none -> 10.3 us  [on_device(): panel_full = pieces.sum(axis=0)]
where the time goes in v1:
time: 407 us
  waiting for transfers between devices  332 us (82%)
  matrix products  30.1 us (7%)
  other arithmetic  15.7 us (4%)
  between operations  14.2 us (3%)
  blocking collectives  13.5 us (3%)
    all_gather x1, waiting for transfers between devices, on_device(): pieces = lax.all_gather(partial_panel, 'col', axis=0, tiled=False)  287 us
    all_gather x1, waiting for transfers between devices, on_device(): portion = lax.all_gather(upper_inverse, 'row', axis=2, tiled=True)  44.1 us
    dot_general x8, matrix products, single(): jnp.einsum(pattern, left, right, precision=lax.Precision.HIGHEST, preferr...  30.1 us
    psum x1, blocking collectives, on_device(): entries = lax.psum(partial_entries, 'col')  13.5 us
    reduce_sum x1, other arithmetic, on_device(): panel_full = pieces.sum(axis=0)  10.3 us
  transfers between devices with their start and end apart: 2, of which 2 were waited for; matrix products, arithmetic and copies ran while one was open for 1% of the time, Pallas kernels for 0%

profile of v1, /device:TPU:0, one launch (start us, length us, event | category | flops | bytes accessed | tf_op | source)
XLA Modules:
  0.0 407.1 jit_solution(6345910337277277794)
XLA Ops:
  7.2 0.0 all-gather.4.cloned.1.call-start
  7.2 0.7 all-gather.4.cloned.1.call-update
  7.9 0.0 all-gather.6.cloned.1.call-start
  8.0 0.8 compare_convert_fusion
  8.8 0.0 copy-start.3
  8.8 1.4 fusion.20
  10.2 13.5 %psum.7 = f32[2,2,128]{2,1,0:T(2,128)S(1)} all-reduce(f32[2,2,128]{2,1,0:T(2,128)S(1)} %fusion.20), channel_id=1, replica_groups=mesh['row'=8,'col'=4] {'col'}, use_global_device_ids=true, to_apply=%region_1.0 | all-reduce | flops 512 | bytes 4096 | tf_op jit(solution)/shard_map/psum | solution.py:41
  23.7 0.7 broadcast_multiply_fusion
  24.3 0.1 select_divide_fusion
  24.4 44.1 %all-gather.4.cloned.1.call-done = f32[2,512,2048]{2,1,0:T(8,128)} async-done(((f32[2,512,256]{2,1,0:T(8,128)}), f32[2,512,2048]{2,1,0:T(8,128)}) %all-gather.4.cloned.1.call-update) | async-done | bytes 8388624 | tf_op jit(solution)/shard_map/all_gather | solution.py:48
  68.5 0.0 copy-start.1
  68.5 5.9 %fusion = f32[2,128,2048]{2,1,0:T(8,128)S(1)} fusion(f32[2,512,2048]{2,1,0:T(8,128)} %all-gather.4.cloned.1.call-done, f32[2,2,128,512]{3,2,1,0:T(8,128)} %param.7, f32[2,128]{1,0:T(2,128)S(1)} %get-tuple-element.7, f32[2,128]{1,0:T(2,128)S(1)} %get-tuple-element.6), kind=kOutput, calls=%fused_computation.3 | convolution fusion | flops 3221618688 | bytes 7342080 | tf_op jit(solution)/shard_map/trk,kn->trn/dot_general | solution.py:12
  74.4 0.0 copy-done.3
  74.4 5.7 %fusion.1 = f32[2,128,2048]{2,1,0:T(8,128)S(1)} fusion(f32[2,512,2048]{2,1,0:T(8,128)} %all-gather.4.cloned.1.call-done, f32[2,2,128,512]{3,2,1,0:T(8,128)S(1)} %copy-done.3, f32[2,128]{1,0:T(2,128)S(1)} %get-tuple-element.7, f32[2,128]{1,0:T(2,128)S(1)} %get-tuple-element.6), kind=kOutput, calls=%fused_computation.4 | convolution fusion | flops 3221618688 | bytes 7342080 | tf_op jit(solution)/shard_map/trk,kn->trn/dot_general | solution.py:12
  80.1 0.0 copy-done.1
  80.1 3.8 fusion.7
  84.0 3.8 fusion.5
  87.8 2.4 pad_maximum_fusion
  90.2 0.0 all-gather.6.cloned.1.call-update
  90.2 286.9 %all-gather.6.cloned.1.call-done = f32[8,2,128,2048]{3,2,0,1:T(8,128)} async-done(((f32[2,2,128,2048]{3,2,0,1:T(8,128)}), f32[8,2,128,2048]{3,2,0,1:T(8,128)}) %all-gather.6.cloned.1.call-update) | async-done | bytes 16777232 | tf_op jit(solution)/shard_map/all_gather | solution.py:53
  377.1 0.0 copy-start.2
  377.1 10.3 %reduce_sum.19 = f32[2,2,128,2048]{3,2,0,1:T(8,128)} reduce(f32[4,2,2,128,2048]{4,3,1,0,2:T(8,128)} %bitcast.87, f32[]{:T(128)} %constant.4.clone.1), dimensions={0}, to_apply=%region_2.0 | reduce | flops 3145728 | bytes 20971524 | tf_op jit(solution)/shard_map/reduce_sum | solution.py:54
  387.4 0.0 copy-done.2
  387.4 0.0 copy-start
  387.4 3.5 fusion.8
  391.0 3.6 fusion.9
  394.6 0.0 copy-done
  394.6 1.8 fusion.15
  396.5 1.8 fusion.13
  398.3 0.1 constant_dynamic-slice_fusion
  398.4 1.0 copy.11
  399.5 0.7 copy.12
  (3 shorter events, 0.0 us)
Async XLA Ops:
  7.2 61.3 %all-gather.4.cloned.1.call-start = ((), (), s32[]{:S(2)}) async-start(), calls=%async_computation | async-start | bytes 9437184 | tf_op jit(solution)/shard_map/all_gather | solution.py:48
  7.9 369.2 %all-gather.6.cloned.1.call-start = ((), (), s32[]{:S(2)}) async-start(), calls=%async_computation.1 | async-start | bytes 20971520 | tf_op jit(solution)/shard_map/all_gather | solution.py:53
  8.8 65.6 %copy-start.3 = (f32[2,2,128,512]{3,2,1,0:T(8,128)S(1)}, f32[2,2,128,512]{3,2,1,0:T(8,128)}, u32[]{:S(2)}) copy-start(f32[2,2,128,512]{3,2,1,0:T(8,128)} %param.7) | copy-start | bytes 3145732
  68.5 11.7 %copy-start.1 = (f32[2,512,2048]{2,1,0:T(8,128)S(1)}, f32[2,512,2048]{2,1,0:T(8,128)}, u32[]{:S(2)}) copy-start(f32[2,512,2048]{2,1,0:T(8,128)} %all-gather.4.cloned.1.call-done) | copy-start | bytes 25165828
  377.1 10.3 %copy-start.2 = (f32[1,2,2048,128]{3,2,1,0:T(8,128)S(1)}, f32[1,2,2048,128]{3,2,1,0:T(8,128)}, u32[]{:S(2)}) copy-start(f32[1,2,2048,128]{3,2,1,0:T(8,128)} %param.11) | copy-start | bytes 6291460
  387.4 7.2 %copy-start = (f32[2,2,128,2048]{3,2,0,1:T(8,128)S(1)}, f32[2,2,128,2048]{3,2,0,1:T(8,128)}, u32[]{:S(2)}) copy-start(f32[2,2,128,2048]{3,2,0,1:T(8,128)} %reduce_sum.19) | copy-start | bytes 12582916
Sparse Core Ops, SparseCore 0:
  9.8 58.5 all-gather.3
  90.4 286.7 all-gather.5
